TPU v7x, 32 devices: a whole 2x2x4 slice. The times are simulated.
32 devices in a mesh: groups: 2 (over y), seq: 4 (over z), proj: 2 (over x), chan: 2 (over core).
Axes of the slice: x: 2, y: 2, z: 4, core: 2. Of those that a mesh axis runs over, the one named last changes fastest.
Arguments:
- tokens: bfloat16 [8192, 8192], P('seq', ('proj', 'chan')), may hold values from -6 to 6
- w_proj: bfloat16 [8192, 3, 512], P('proj', None, ('groups', 'chan')), parts along dimension 2, may hold values from -0.0625 to 0.0625
- short_taps: float32 [3, 3, 512], P(None, None, ('groups', 'chan')), parts along dimension 2, may hold values from -3 to 3
- long_filter: bfloat16 [8192, 512], P(('seq', 'proj'), ('groups', 'chan')), parts along dimension 1, may hold values from -0.0625 to 0.0625
- filter_bias: float32 [512], P(('groups', 'chan')), parts along dimension 0, may hold values from -1 to 1
Outputs:
- mixed: bfloat16 [8192, 512], P(('seq', 'proj'), ('groups', 'chan')), parts along dimension 1
There are 2 independent parts, one for each index of `groups`. A program takes and returns all parts, laid end to end along the dimension named above; an argument that names none is the same for every part. Nothing has to cross between parts.
All inputs are finite; a program needn't handle non-finite values.
Results may differ from a plain program's by a relative error of at most 0.0075.
Values may be sent and summed in bfloat16 or wider, within the bound.
No kernel may reach another device: no remote copies, remote signals or barrier semaphores. Data moves between devices by JAX's collectives and lax.ppermute only.
A program may use at most 128 MiB of HBM per device.

v0:
```python
import math
import jax
import jax.numpy as jnp
from jax import lax
from jax.sharding import PartitionSpec as P

precise = lax.Precision.HIGH


def shifted(array, axis, by):
    size = lax.axis_size(axis)
    pairs = [(i, i + by) for i in range(size) if 0 <= i + by < size]
    return lax.ppermute(array, axis, pairs)


def twist_angles(outer, inner, total):
    outer_ids = lax.broadcasted_iota(jnp.int32, (outer, inner), 0)
    inner_ids = lax.broadcasted_iota(jnp.int32, (outer, inner), 1)
    return (outer_ids * inner_ids % total).astype(jnp.float32) * (2.0 * math.pi / total)


def dft_tables(points, direction):
    phases = twist_angles(points, points, points)
    return (jnp.cos(phases), direction * jnp.sin(phases))


def complex_einsum(form, left_re, left_im, right_re, right_im):
    real_out = jnp.einsum(form, left_re, right_re, precision=precise) - jnp.einsum(
        form, left_im, right_im, precision=precise
    )
    imag_out = jnp.einsum(form, left_re, right_im, precision=precise) + jnp.einsum(
        form, left_im, right_re, precision=precise
    )
    return (real_out, imag_out)


def rotate(data_re, data_im, turn_angle):
    cosine = jnp.cos(turn_angle)
    sine_part = jnp.sin(turn_angle)
    return (data_re * cosine - data_im * sine_part, data_re * sine_part + data_im * cosine)


def spectral_product(data_re, data_im, width, along):
    first_re = lax.slice_in_dim(data_re, 0, 2 * width, axis=along)
    first_im = lax.slice_in_dim(data_im, 0, 2 * width, axis=along)
    second_re = lax.slice_in_dim(data_re, 2 * width, 4 * width, axis=along)
    second_im = lax.slice_in_dim(data_im, 2 * width, 4 * width, axis=along)
    return (
        first_re * second_re - first_im * second_im,
        first_re * second_im + first_im * second_re,
    )


def combine_halves(time_re, time_im, width, turn_angle, along):
    even_part = lax.slice_in_dim(time_re, 0, width, axis=along)
    odd_re = lax.slice_in_dim(time_re, width, 2 * width, axis=along)
    odd_im = lax.slice_in_dim(time_im, width, 2 * width, axis=along)
    return 0.5 * (even_part + jnp.cos(turn_angle) * odd_re - jnp.sin(turn_angle) * odd_im)


def shards(tokens, w_proj, short_taps, long_filter, filter_bias):
    whole_cols = lax.all_gather(tokens, "chan", axis=1, tiled=True)
    width_in, triple, channels = w_proj.shape
    weights = w_proj.reshape(width_in, triple * channels)
    parts_proj = lax.axis_size("proj")
    rows_own = tokens.shape[0] // parts_proj
    projected = lax.psum_scatter(
        jnp.dot(whole_cols, weights, preferred_element_type=jnp.float32),
        "proj",
        scatter_dimension=0,
        tiled=True,
    )
    tap_count = short_taps.shape[0]
    taps_flat = short_taps.reshape(tap_count, triple * channels)
    tail_rows = projected[rows_own - (tap_count - 1) :]
    earlier = shifted(tail_rows, ("seq", "proj"), 1)
    extended = jnp.concatenate([earlier, projected], axis=0)
    featured = taps_flat[0] * projected
    for lag_step in range(1, tap_count):
        featured = (
            featured
            + taps_flat[lag_step]
            * extended[tap_count - 1 - lag_step : tap_count - 1 - lag_step + rows_own]
        )
    query_part = featured[:, :channels]
    gated_low = (featured[:, channels : 2 * channels] * featured[:, 2 * channels :]).astype(
        jnp.bfloat16
    )
    gated_rows = gated_low.astype(jnp.float32)
    devices = lax.axis_size(("seq", "proj"))
    seq_len = devices * rows_own
    per_device = channels // devices
    gated_low_cols, filter_low_cols = (
        lax.all_to_all(gated_low.T, ("seq", "proj"), split_axis=0, concat_axis=1, tiled=True),
        lax.all_to_all(long_filter.T, ("seq", "proj"), split_axis=0, concat_axis=1, tiled=True),
    )
    gated_cols = gated_low_cols.astype(jnp.float32)
    filter_cols = filter_low_cols.astype(jnp.float32)
    full_angle = lax.broadcasted_iota(jnp.int32, (1, seq_len), 1).astype(jnp.float32) * (
        math.pi / seq_len
    )
    zero_cols = jnp.zeros_like(gated_cols)
    umod_re, umod_im = rotate(gated_cols, zero_cols, -full_angle)
    hmod_re, hmod_im = rotate(filter_cols, zero_cols, -full_angle)
    series_re = jnp.concatenate([gated_cols, umod_re, filter_cols, hmod_re], axis=0)
    series_im = jnp.concatenate([zero_cols, umod_im, zero_cols, hmod_im], axis=0)
    grid_re = series_re.reshape(4 * per_device, devices, rows_own)
    grid_im = series_im.reshape(4 * per_device, devices, rows_own)
    outer_re, outer_im = dft_tables(devices, -1.0)
    inner_re, inner_im = dft_tables(rows_own, -1.0)
    twist = twist_angles(devices, rows_own, seq_len)
    grid_re, grid_im = complex_einsum("kd,cdj->ckj", outer_re, outer_im, grid_re, grid_im)
    grid_re, grid_im = rotate(grid_re, grid_im, -twist)
    grid_re, grid_im = complex_einsum("ckj,jq->ckq", grid_re, grid_im, inner_re, inner_im)
    spec_re, spec_im = spectral_product(grid_re, grid_im, per_device, 0)
    back_inner_re, back_inner_im = dft_tables(rows_own, 1.0)
    back_outer_re, back_outer_im = dft_tables(devices, 1.0)
    back_re, back_im = complex_einsum("ckq,qj->ckj", spec_re, spec_im, back_inner_re, back_inner_im)
    back_re, back_im = rotate(back_re, back_im, twist)
    back_re, back_im = complex_einsum("dk,ckj->cdj", back_outer_re, back_outer_im, back_re, back_im)
    time_re = back_re.reshape(2 * per_device, seq_len) * (1.0 / seq_len)
    time_im = back_im.reshape(2 * per_device, seq_len) * (1.0 / seq_len)
    long_cols = combine_halves(time_re, time_im, per_device, full_angle, 0)
    long_rows = lax.all_to_all(long_cols, ("seq", "proj"), split_axis=1, concat_axis=0, tiled=True)
    long_conv = long_rows.T
    result = query_part * (long_conv + filter_bias * gated_rows)
    return result.astype(jnp.bfloat16)


def solution(mesh):
    placed = (
        P("seq", ("proj", "chan")),
        P("proj", None, ("groups", "chan")),
        P(None, None, ("groups", "chan")),
        P(("seq", "proj"), ("groups", "chan")),
        P(("groups", "chan")),
    )
    return jax.shard_map(
        shards,
        mesh=mesh,
        in_specs=placed,
        out_specs=P(("seq", "proj"), ("groups", "chan")),
        check_vma=False,
    )
```

profile of v0, /device:TPU:0, one launch (start us, length us, event | category | flops | bytes accessed | tf_op | source)
XLA Modules:
  0.0 312.7 jit_solution(15190194606105853624)
XLA Ops:
  6.5 0.7 all-gather.2.cloned.1.call-update
  7.3 1.1 copy-done
  8.4 2.9 copy.14
  11.3 30.4 %all-gather.2.cloned.1.call-done = bf16[2048,4096]{1,0:T(8,128)(2,1)} async-done(((bf16[2048,2048]{1,0:T(8,128)(2,1)}), bf16[2048,4096]{1,0:T(8,128)(2,1)}) %all-gather.2.cloned.1.call-update) | async-done | bytes 16777232 | tf_op jit(solution)/shard_map/all_gather | solution.py:62
  41.7 14.5 %fusion.186 = f32[2048,384]{1,0:T(8,128)} fusion(bf16[2048,4096]{1,0:T(8,128)(2,1)} %all-gather.2.cloned.1.call-done, bf16[4096,384]{0,1:T(8,128)(2,1)} %bitcast.120), kind=kOutput, calls=%fused_computation.202 | convolution fusion | flops 6442450944 | bytes 23068672 | tf_op jit(solution)/shard_map/dot_general | solution.py:68
  56.2 0.9 copy.17
  57.1 5.8 %all-to-all-start.1 = ((bf16[8,16,1024]{2,1,0:T(8,128)(2,1)}), bf16[8,16,1024]{2,1,0:T(8,128)(2,1)S(1)}, u32[]{:S(2)}, u32[]{:S(2)}) async-start(bf16[8,16,1024]{2,1,0:T(8,128)(2,1)} %bitcast.8), calls=%async_computation.2 | async-start | bytes 524288 | tf_op jit(solution)/shard_map/all_to_all | solution.py:95
  63.2 40.5 %reduce-scatter.2.cloned.1.call-done = f32[1024,384]{1,0:T(8,128)} async-done(((f32[2048,384]{1,0:T(8,128)}), f32[1024,384]{1,0:T(8,128)}) %reduce-scatter.2.cloned.1.call-update) | async-done | bytes 1572880 | tf_op jit(solution)/shard_map/reduce_scatter | solution.py:67
  104.4 2.2 collective-permute-start
  106.8 1.1 collective-permute-done
  107.9 3.2 %fusion.45 = f32[1024,384]{1,0:T(8,128)S(1)} fusion(f32[2,384]{1,0:T(2,128)S(1)} %collective-permute-done, f32[1024,384]{1,0:T(8,128)} %reduce-scatter.2.cloned.1.call-done, f32[384]{0:T(512)S(1)} %get-tuple-element.16, f32[384]{0:T(512)S(1)} %get-tuple-element.17, f32[384]{0:T(512)S(1)} %get-tuple-element.15), kind=kLoop, calls=%fused_computation.48 | loop fusion | flops 2752512 | bytes 3153408 | tf_op jit(solution)/shard_map/add | solution.py:81
  111.2 0.8 copy.15
  112.1 8.0 %all-to-all-start = ((bf16[8,16,1024]{2,1,0:T(8,128)(2,1)}), bf16[8,16,1024]{2,1,0:T(8,128)(2,1)S(1)}, u32[]{:S(2)}, u32[]{:S(2)}) async-start(bf16[8,16,1024]{2,1,0:T(8,128)(2,1)} %bitcast.5), calls=%async_computation.1 | async-start | bytes 524288 | tf_op jit(solution)/shard_map/all_to_all | solution.py:94
  120.5 7.3 %all-to-all-done = bf16[8,16,1024]{2,1,0:T(8,128)(2,1)S(1)} async-done(((bf16[8,16,1024]{2,1,0:T(8,128)(2,1)}), bf16[8,16,1024]{2,1,0:T(8,128)(2,1)S(1)}, u32[]{:S(2)}, u32[]{:S(2)}) %all-to-all-start) | async-done | bytes 262176 | tf_op jit(solution)/shard_map/all_to_all | solution.py:94
  128.3 1.2 fusion.63
  129.5 1.2 fusion.64
  130.8 1.3 fusion.41
  132.2 1.3 fusion.40
  133.5 19.1 %fusion.7 = f32[64,8,1024]{2,1,0:T(8,128)S(1)} fusion(f32[64,1024,8]{1,2,0:T(8,128)S(1)} %fusion.41, f32[64,1024,8]{1,2,0:T(8,128)S(1)} %fusion.40, f32[8,1024]{1,0:T(8,128)S(1)} %get-tuple-element.22, f32[8,1024]{1,0:T(8,128)S(1)} %get-tuple-element.23), kind=kOutput, calls=%fused_computation.10 | convolution fusion | flops 3238526976 | bytes 6356992 | tf_op jit(solution)/shard_map/ckj,jq->ckq/dot_general | solution.py:31
  152.6 19.1 %fusion.9 = f32[64,8,1024]{2,1,0:T(8,128)S(1)} fusion(f32[64,1024,8]{1,2,0:T(8,128)S(1)} %fusion.41, f32[64,1024,8]{1,2,0:T(8,128)S(1)} %fusion.40, f32[8,1024]{1,0:T(8,128)S(1)} %get-tuple-element.22, f32[8,1024]{1,0:T(8,128)S(1)} %get-tuple-element.23), kind=kOutput, calls=%fused_computation.12 | convolution fusion | flops 3238526976 | bytes 6356992 | tf_op jit(solution)/shard_map/ckj,jq->ckq/dot_general | solution.py:28
  171.7 18.8 %fusion.50 = f32[64,8,1024]{2,1,0:T(8,128)S(1)} fusion(f32[64,8,1024]{2,1,0:T(8,128)S(1)} %fusion.7, f32[64,1024,8]{1,2,0:T(8,128)S(1)} %fusion.41, f32[64,1024,8]{1,2,0:T(8,128)S(1)} %fusion.40, f32[8,1024]{1,0:T(8,128)S(1)} %get-tuple-element.22, f32[8,1024]{1,0:T(8,128)S(1)} %get-tuple-element.23), kind=kOutput, calls=%fused_computation.52 | convolution fusion | flops 3238002688 | bytes 8454144 | tf_op jit(solution)/shard_map/ckj,jq->ckq/dot_general | solution.py:31
  190.6 18.8 %fusion.47 = f32[64,8,1024]{2,1,0:T(8,128)S(1)} fusion(f32[64,8,1024]{2,1,0:T(8,128)S(1)} %fusion.9, f32[64,1024,8]{1,2,0:T(8,128)S(1)} %fusion.41, f32[64,1024,8]{1,2,0:T(8,128)S(1)} %fusion.40, f32[8,1024]{1,0:T(8,128)S(1)} %get-tuple-element.22, f32[8,1024]{1,0:T(8,128)S(1)} %get-tuple-element.23), kind=kOutput, calls=%fused_computation.51 | convolution fusion | flops 3238002688 | bytes 8454144 | tf_op jit(solution)/shard_map/ckj,jq->ckq/dot_general | solution.py:28
  209.9 18.4 %fusion.3 = f32[32,8,1024]{2,1,0:T(8,128)S(1)} fusion(f32[32,8,1024]{2,1,0:T(8,128)S(1)} %get-tuple-element.6), kind=kOutput, calls=%fused_computation.6 | convolution fusion | flops 1625292800 | bytes 2097152 | tf_op jit(solution)/shard_map/ckq,qj->ckj/dot_general | solution.py:31
  228.3 18.2 %fusion.5 = f32[32,8,1024]{2,1,0:T(8,128)S(1)} fusion(f32[32,8,1024]{2,1,0:T(8,128)S(1)} %get-tuple-element.5), kind=kOutput, calls=%fused_computation.8 | convolution fusion | flops 1625292800 | bytes 2097152 | tf_op jit(solution)/shard_map/ckq,qj->ckj/dot_general | solution.py:28
  246.6 18.3 %fusion.60 = f32[32,8,1024]{2,1,0:T(8,128)S(1)} fusion(f32[32,8,1024]{2,1,0:T(8,128)S(1)} %fusion.3, f32[32,8,1024]{2,1,0:T(8,128)S(1)} %get-tuple-element.5), kind=kOutput, calls=%fused_computation.60 | convolution fusion | flops 1625554944 | bytes 3145728 | tf_op jit(solution)/shard_map/ckq,qj->ckj/dot_general | solution.py:31
  264.9 18.4 %fusion.57 = f32[32,8,1024]{2,1,0:T(8,128)S(1)} fusion(f32[32,8,1024]{2,1,0:T(8,128)S(1)} %fusion.5, f32[32,8,1024]{2,1,0:T(8,128)S(1)} %get-tuple-element.6), kind=kOutput, calls=%fused_computation.59 | convolution fusion | flops 1625554944 | bytes 3145728 | tf_op jit(solution)/shard_map/ckq,qj->ckj/dot_general | solution.py:28
  283.3 0.7 fusion.72
  284.0 0.7 fusion.71
  284.8 0.8 fusion.54
  286.0 0.8 fusion.56
  287.7 16.9 %all_to_all.45 = f32[16,8,1024]{2,0,1:T(8,128)S(1)} all-to-all(f32[16,8,1024]{2,0,1:T(8,128)S(1)} %bitcast.122), channel_id=1, replica_groups=mesh['groups'=2,'seq'=4,'proj'=2,'chan'=2] {'seq','proj'}, dimensions={1} | all-to-all | bytes 1048576 | tf_op jit(solution)/shard_map/all_to_all | solution.py:124
  304.8 0.8 fusion.70
  (32 shorter events, 4.1 us)
Async XLA Ops:
  6.5 1.9 copy-start
  6.5 35.2 %all-gather.2.cloned.1.call-start = ((), (), s32[]{:S(2)}) async-start(), calls=%async_computation.4 | async-start | bytes 25165824 | tf_op jit(solution)/shard_map/all_gather | solution.py:62
  7.3 96.5 %reduce-scatter.2.cloned.1.call-start = ((), (), s32[]{:S(2)}) async-start(), calls=%async_computation.5 | async-start | bytes 4718592 | tf_op jit(solution)/shard_map/reduce_scatter | solution.py:67
  41.7 14.5 %copy-start.1 = (bf16[1024,128]{1,0:T(8,128)(2,1)S(1)}, bf16[1024,128]{1,0:T(8,128)(2,1)}, u32[]{:S(2)}) copy-start(bf16[1024,128]{1,0:T(8,128)(2,1)} %param.8) | copy-start | bytes 786436
  56.2 6.9 %copy-start.2 = (f32[3,3,128]{2,1,0:T(4,128)S(1)}, f32[3,3,128]{2,1,0:T(4,128)}, u32[]{:S(2)}) copy-start(f32[3,3,128]{2,1,0:T(4,128)} %param.7) | copy-start | bytes 13828
  57.1 55.0 %all-to-all-start.1 = ((bf16[8,16,1024]{2,1,0:T(8,128)(2,1)}), bf16[8,16,1024]{2,1,0:T(8,128)(2,1)S(1)}, u32[]{:S(2)}, u32[]{:S(2)}) async-start(bf16[8,16,1024]{2,1,0:T(8,128)(2,1)} %bitcast.8), calls=%async_computation.2 | async-start | bytes 524288 | tf_op jit(solution)/shard_map/all_to_all | solution.py:95
  104.4 3.5 %collective-permute-start = (f32[2,384]{1,0:T(2,128)S(1)}, f32[2,384]{1,0:T(2,128)S(1)}, u32[]{:S(2)}, u32[]{:S(2)}) collective-permute-start(f32[2,384]{1,0:T(2,128)S(1)} %slice.79), channel_id=1, source_target_pairs={{0,2},{2,4},{4,6},{6,8},{8,10},{10,12},{12,14},{1,3},{3,5},{5,7},{... | collective-permute-start | bytes 9224 | tf_op jit(solution)/shard_map/ppermute | solution.py:13
  112.1 15.7 %all-to-all-start = ((bf16[8,16,1024]{2,1,0:T(8,128)(2,1)}), bf16[8,16,1024]{2,1,0:T(8,128)(2,1)S(1)}, u32[]{:S(2)}, u32[]{:S(2)}) async-start(bf16[8,16,1024]{2,1,0:T(8,128)(2,1)} %bitcast.5), calls=%async_computation.1 | async-start | bytes 524288 | tf_op jit(solution)/shard_map/all_to_all | solution.py:94
  286.9 17.9 %copy-start.3 = (f32[128]{0:T(128)S(1)}, f32[128]{0:T(128)}, u32[]{:S(2)}) copy-start(f32[128]{0:T(128)} %param.9) | copy-start | bytes 1540
Sparse Core Ops, SparseCore 0:
  8.9 32.7 all-gather.1
  56.4 47.3 reduce-scatter.1
where the time goes:
time: 317 us; the launch traced here: 313 us
  matrix products  172 us (54%)
  waiting for transfers between devices  80.1 us (25%)
  blocking collectives  16.9 us (5%)
  starting transfers between devices  16 us (5%)
  between operations  14 us (4%)
  local copies, waits for them, and re-layouts  7.73 us (2%)
  other arithmetic  6.06 us (2%)
    reduce_scatter x1, waiting for transfers between devices, shards(): lax.psum_scatter(jnp.dot(whole_cols, weights, preferred_element_type=jnp....  40.5 us
    dot_general x4, matrix products, complex_einsum(): jnp.einsum(form, left_re, right_im, precision=precise)  39.6 us
    dot_general x4, matrix products, complex_einsum(): jnp.einsum(form, left_im, right_im, precision=precise)  39.5 us
    dot_general x4, matrix products, complex_einsum(): jnp.einsum(form, left_re, right_re, precision=precise)  39.2 us
    dot_general x4, matrix products, complex_einsum(): jnp.einsum(form, left_im, right_re, precision=precise)  39.2 us
    all_gather x1, waiting for transfers between devices, shards(): whole_cols = lax.all_gather(tokens, 'chan', axis=1, tiled=True)  30.4 us
    all_to_all x1, blocking collectives, shards(): lax.all_to_all(long_cols, ('seq', 'proj'), split_axis=1, concat_axis=0, t...  16.9 us
    dot_general x1, matrix products, shards(): jnp.dot(whole_cols, weights, preferred_element_type=jnp.float32)  14.5 us
  transfers between devices with their start and end apart: 5, of which 4 were waited for; matrix products, arithmetic and copies ran while one was open for 3% of the time, Pallas kernels for 0%

commit v1 on v0

--- a/solution.py
+++ b/solution.py
@@ -5,6 +5,22 @@
 from jax.sharding import PartitionSpec as P
 
 precise = lax.Precision.HIGH
+
+
+def exchange_in_pairs(x, axis, split, join):
+    ways, here = (lax.axis_size(axis), lax.axis_index(axis))
+    width = x.shape[split] // ways
+    shape = list(x.shape)
+    shape[split] = width
+    height = shape[join]
+    shape[join] = height * ways
+    full = jnp.zeros(shape, x.dtype)
+    for mask in range(ways):
+        part = lax.dynamic_slice_in_dim(x, (here ^ mask) * width, width, axis=split)
+        if mask:
+            part = lax.ppermute(part, axis, [(d, d ^ mask) for d in range(ways)])
+        full = lax.dynamic_update_slice_in_dim(full, part, (here ^ mask) * height, axis=join)
+    return full
 
 
 def shifted(array, axis, by):
@@ -121,7 +137,7 @@
     time_re = back_re.reshape(2 * per_device, seq_len) * (1.0 / seq_len)
     time_im = back_im.reshape(2 * per_device, seq_len) * (1.0 / seq_len)
     long_cols = combine_halves(time_re, time_im, per_device, full_angle, 0)
-    long_rows = lax.all_to_all(long_cols, ("seq", "proj"), split_axis=1, concat_axis=0, tiled=True)
+    long_rows = exchange_in_pairs(long_cols, ("seq", "proj"), 1, 0)
     long_conv = long_rows.T
     result = query_part * (long_conv + filter_bias * gated_rows)
     return result.astype(jnp.bfloat16)

time: 317 us -> 415 us (1.31)
  the two profiles are of different devices: /device:TPU:0 before, /device:TPU:16 now
where the time goes in v1:
time: 415 us; the launch traced here: 410 us
  matrix products  172 us (41%)
  waiting for transfers between devices  137 us (33%)
  local copies, waits for them, and re-layouts  52.2 us (13%)
  starting transfers between devices  21.8 us (5%)
  between operations  14 us (3%)
  other arithmetic  13.4 us (3%)
    ppermute x7, waiting for transfers between devices, exchange_in_pairs(): part = lax.ppermute(part, axis, [(d, d ^ mask) for d in range(ways)])  57.5 us
    reduce_scatter x1, waiting for transfers between devices, shards(): lax.psum_scatter(jnp.dot(whole_cols, weights, preferred_element_type=jnp....  40 us
    dot_general x4, matrix products, complex_einsum(): jnp.einsum(form, left_re, right_im, precision=precise)  39.9 us
    dot_general x4, matrix products, complex_einsum(): jnp.einsum(form, left_im, right_re, precision=precise)  39.6 us
    dot_general x4, matrix products, complex_einsum(): jnp.einsum(form, left_im, right_im, precision=precise)  39.2 us
    dot_general x4, matrix products, complex_einsum(): jnp.einsum(form, left_re, right_re, precision=precise)  38.7 us
    dynamic_update_slice x8, local copies, waits for them, and re-layouts, exchange_in_pairs(): lax.dynamic_update_slice_in_dim(full, part, (here ^ mask) * height, axis=...  32.3 us
    all_gather x1, waiting for transfers between devices, shards(): whole_cols = lax.all_gather(tokens, 'chan', axis=1, tiled=True)  29.1 us
  transfers between devices with their start and end apart: 12, of which 9 were waited for; matrix products, arithmetic and copies ran while one was open for 9% of the time, Pallas kernels for 0%

profile of v1, /device:TPU:16, one launch (start us, length us, event | category | flops | bytes accessed | tf_op | source)
XLA Modules:
  0.0 410.0 jit_solution(14977432995523463204)
XLA Ops:
  8.4 2.8 copy.18
  11.3 29.1 %all-gather.2.cloned.1.call-done = bf16[2048,4096]{1,0:T(8,128)(2,1)} async-done(((bf16[2048,2048]{1,0:T(8,128)(2,1)}), bf16[2048,4096]{1,0:T(8,128)(2,1)}) %all-gather.2.cloned.1.call-update) | async-done | bytes 16777232 | tf_op jit(solution)/shard_map/all_gather | solution.py:78
  40.4 14.5 %fusion.189 = f32[2048,384]{1,0:T(8,128)} fusion(bf16[2048,4096]{1,0:T(8,128)(2,1)} %all-gather.2.cloned.1.call-done, bf16[4096,384]{0,1:T(8,128)(2,1)} %bitcast.121), kind=kOutput, calls=%fused_computation.213 | convolution fusion | flops 6442450944 | bytes 23068672 | tf_op jit(solution)/shard_map/dot_general | solution.py:84
  55.7 6.0 %all-to-all-start.1 = ((bf16[8,16,1024]{2,1,0:T(8,128)(2,1)}), bf16[8,16,1024]{2,1,0:T(8,128)(2,1)S(1)}, u32[]{:S(2)}, u32[]{:S(2)}) async-start(bf16[8,16,1024]{2,1,0:T(8,128)(2,1)} %bitcast.8), calls=%async_computation.2 | async-start | bytes 524288 | tf_op jit(solution)/shard_map/all_to_all | solution.py:111
  62.1 40.0 %reduce-scatter.2.cloned.1.call-done = f32[1024,384]{1,0:T(8,128)} async-done(((f32[2048,384]{1,0:T(8,128)}), f32[1024,384]{1,0:T(8,128)}) %reduce-scatter.2.cloned.1.call-update) | async-done | bytes 1572880 | tf_op jit(solution)/shard_map/reduce_scatter | solution.py:83
  105.5 3.7 collective-permute-done
  109.2 3.0 fusion.48
  114.2 5.3 %all-to-all-start = ((bf16[8,16,1024]{2,1,0:T(8,128)(2,1)}), bf16[8,16,1024]{2,1,0:T(8,128)(2,1)S(1)}, u32[]{:S(2)}, u32[]{:S(2)}) async-start(bf16[8,16,1024]{2,1,0:T(8,128)(2,1)} %bitcast.5), calls=%async_computation.1 | async-start | bytes 524288 | tf_op jit(solution)/shard_map/all_to_all | solution.py:110
  120.0 5.5 %all-to-all-done = bf16[8,16,1024]{2,1,0:T(8,128)(2,1)S(1)} async-done(((bf16[8,16,1024]{2,1,0:T(8,128)(2,1)}), bf16[8,16,1024]{2,1,0:T(8,128)(2,1)S(1)}, u32[]{:S(2)}, u32[]{:S(2)}) %all-to-all-start) | async-done | bytes 262176 | tf_op jit(solution)/shard_map/all_to_all | solution.py:110
  131.2 19.3 %fusion.10 = f32[64,8,1024]{2,1,0:T(8,128)S(1)} fusion(f32[64,1024,8]{1,2,0:T(8,128)S(1)} %fusion.44, f32[64,1024,8]{1,2,0:T(8,128)S(1)} %fusion.43, f32[8,1024]{1,0:T(8,128)S(1)} %get-tuple-element.30, f32[8,1024]{1,0:T(8,128)S(1)} %get-tuple-element.31), kind=kOutput, calls=%fused_computation.15 | convolution fusion | flops 3238526976 | bytes 6356992 | tf_op jit(solution)/shard_map/ckj,jq->ckq/dot_general | solution.py:47
  150.6 18.9 %fusion.12 = f32[64,8,1024]{2,1,0:T(8,128)S(1)} fusion(f32[64,1024,8]{1,2,0:T(8,128)S(1)} %fusion.44, f32[64,1024,8]{1,2,0:T(8,128)S(1)} %fusion.43, f32[8,1024]{1,0:T(8,128)S(1)} %get-tuple-element.30, f32[8,1024]{1,0:T(8,128)S(1)} %get-tuple-element.31), kind=kOutput, calls=%fused_computation.17 | convolution fusion | flops 3238526976 | bytes 6356992 | tf_op jit(solution)/shard_map/ckj,jq->ckq/dot_general | solution.py:44
  169.5 19.0 %fusion.53 = f32[64,8,1024]{2,1,0:T(8,128)S(1)} fusion(f32[64,8,1024]{2,1,0:T(8,128)S(1)} %fusion.10, f32[64,1024,8]{1,2,0:T(8,128)S(1)} %fusion.44, f32[64,1024,8]{1,2,0:T(8,128)S(1)} %fusion.43, f32[8,1024]{1,0:T(8,128)S(1)} %get-tuple-element.30, f32[8,1024]{1,0:T(8,128)S(1)} %get-tuple-element.31), kind=kOutput, calls=%fused_computation.57 | convolution fusion | flops 3238002688 | bytes 8454144 | tf_op jit(solution)/shard_map/ckj,jq->ckq/dot_general | solution.py:47
  188.5 18.6 %fusion.50 = f32[64,8,1024]{2,1,0:T(8,128)S(1)} fusion(f32[64,8,1024]{2,1,0:T(8,128)S(1)} %fusion.12, f32[64,1024,8]{1,2,0:T(8,128)S(1)} %fusion.44, f32[64,1024,8]{1,2,0:T(8,128)S(1)} %fusion.43, f32[8,1024]{1,0:T(8,128)S(1)} %get-tuple-element.30, f32[8,1024]{1,0:T(8,128)S(1)} %get-tuple-element.31), kind=kOutput, calls=%fused_computation.56 | convolution fusion | flops 3238002688 | bytes 8454144 | tf_op jit(solution)/shard_map/ckj,jq->ckq/dot_general | solution.py:44
  207.6 18.4 %fusion.6 = f32[32,8,1024]{2,1,0:T(8,128)S(1)} fusion(f32[32,8,1024]{2,1,0:T(8,128)S(1)} %get-tuple-element.14), kind=kOutput, calls=%fused_computation.11 | convolution fusion | flops 1625292800 | bytes 2097152 | tf_op jit(solution)/shard_map/ckq,qj->ckj/dot_general | solution.py:47
  226.1 18.2 %fusion.8 = f32[32,8,1024]{2,1,0:T(8,128)S(1)} fusion(f32[32,8,1024]{2,1,0:T(8,128)S(1)} %get-tuple-element.13), kind=kOutput, calls=%fused_computation.13 | convolution fusion | flops 1625292800 | bytes 2097152 | tf_op jit(solution)/shard_map/ckq,qj->ckj/dot_general | solution.py:44
  244.3 18.5 %fusion.63 = f32[32,8,1024]{2,1,0:T(8,128)S(1)} fusion(f32[32,8,1024]{2,1,0:T(8,128)S(1)} %fusion.6, f32[32,8,1024]{2,1,0:T(8,128)S(1)} %get-tuple-element.13), kind=kOutput, calls=%fused_computation.65 | convolution fusion | flops 1625554944 | bytes 3145728 | tf_op jit(solution)/shard_map/ckq,qj->ckj/dot_general | solution.py:47
  262.9 18.1 %fusion.60 = f32[32,8,1024]{2,1,0:T(8,128)S(1)} fusion(f32[32,8,1024]{2,1,0:T(8,128)S(1)} %fusion.8, f32[32,8,1024]{2,1,0:T(8,128)S(1)} %get-tuple-element.14), kind=kOutput, calls=%fused_computation.64 | convolution fusion | flops 1625554944 | bytes 3145728 | tf_op jit(solution)/shard_map/ckq,qj->ckj/dot_general | solution.py:44
  284.2 3.7 copy.25
  294.1 7.7 %fusion.4 = f32[16,8192]{0,1:T(8,128)S(1)} fusion(f32[16,8,1024]{0,2,1:T(8,128)} %copy.25, f32[16,8,1024]{0,2,1:T(8,128)} %copy.24, f32[16,8,1024]{0,2,1:T(8,128)} %copy.23, f32[8192]{0:T(1024)S(1)} %get-tuple-element.34, f32[8192]{0:T(1024)S(1)} %get-tuple-element.35), kind=kLoop, calls=%fused_computation.8 | loop fusion | flops 655360 | bytes 2162688 | tf_op jit(solution)/shard_map/mul | solution.py:74
  309.8 7.2 %collective-permute-done.1 = f32[16,1024]{0,1:T(8,128)S(1)} collective-permute-done((f32[16,1024]{0,1:T(8,128)S(1)}, f32[16,1024]{0,1:T(8,128)S(1)}, u32[]{:S(2)}, u32[]{:S(2)}) %collective-permute-start.1) | collective-permute-done | bytes 65568 | tf_op jit(solution)/shard_map/ppermute | solution.py:21
  318.4 19.2 %collective-permute-done.2 = f32[16,1024]{0,1:T(8,128)S(1)} collective-permute-done((f32[16,1024]{0,1:T(8,128)S(1)}, f32[16,1024]{0,1:T(8,128)S(1)}, u32[]{:S(2)}, u32[]{:S(2)}) %collective-permute-start.2) | collective-permute-done | bytes 65568 | tf_op jit(solution)/shard_map/ppermute | solution.py:21
  338.6 3.1 dynamic_update_slice.24
  341.7 4.5 %dynamic_update_slice.25 = f32[128,1024]{0,1:T(8,128)S(1)} dynamic-update-slice(f32[128,1024]{0,1:T(8,128)S(1)} %dynamic_update_slice.24, f32[16,1024]{0,1:T(8,128)} %copy-done.3, s32[]{:T(128)S(6)} %select_n.132, s32[]{:T(128)} %constant.75.clone.1) | dynamic-update-slice | bytes 131076 | tf_op jit(solution)/shard_map/dynamic_update_slice | solution.py:22
  346.2 4.5 %dynamic_update_slice.26 = f32[128,1024]{0,1:T(8,128)S(1)} dynamic-update-slice(f32[128,1024]{0,1:T(8,128)S(1)} %dynamic_update_slice.25, f32[16,1024]{0,1:T(8,128)} %copy-done.4, s32[]{:T(128)S(6)} %select_n.134, s32[]{:T(128)} %constant.75.clone.1) | dynamic-update-slice | bytes 131076 | tf_op jit(solution)/shard_map/dynamic_update_slice | solution.py:22
  350.7 4.5 %dynamic_update_slice.27 = f32[128,1024]{0,1:T(8,128)S(1)} dynamic-update-slice(f32[128,1024]{0,1:T(8,128)S(1)} %dynamic_update_slice.26, f32[16,1024]{0,1:T(8,128)} %collective-permute-done.3, s32[]{:T(128)S(6)} %select_n.136, s32[]{:T(128)} %constant.75.clone.1) | dynamic-update-slice | bytes 131076 | tf_op jit(solution)/shard_map/dynamic_update_slice | solution.py:22
  355.2 3.9 dynamic_update_slice.28
  359.1 18.7 %collective-permute-done.5 = f32[16,1024]{0,1:T(8,128)} collective-permute-done((f32[16,1024]{0,1:T(8,128)}, f32[16,1024]{0,1:T(8,128)}, u32[]{:S(2)}, u32[]{:S(2)}) %collective-permute-start.5) | collective-permute-done | bytes 65568 | tf_op jit(solution)/shard_map/ppermute | solution.py:21
  377.9 4.4 %dynamic_update_slice.29 = f32[128,1024]{0,1:T(8,128)S(1)} dynamic-update-slice(f32[128,1024]{0,1:T(8,128)S(1)} %dynamic_update_slice.28, f32[16,1024]{0,1:T(8,128)} %collective-permute-done.5, s32[]{:T(128)S(6)} %select_n.140, s32[]{:T(128)} %constant.75.clone.1) | dynamic-update-slice | bytes 131076 | tf_op jit(solution)/shard_map/dynamic_update_slice | solution.py:22
  382.3 7.3 %collective-permute-done.6 = f32[16,1024]{0,1:T(8,128)} collective-permute-done((f32[16,1024]{0,1:T(8,128)}, f32[16,1024]{0,1:T(8,128)}, u32[]{:S(2)}, u32[]{:S(2)}) %collective-permute-start.6) | collective-permute-done | bytes 65568 | tf_op jit(solution)/shard_map/ppermute | solution.py:21
  389.6 4.4 %dynamic_update_slice.30 = f32[128,1024]{0,1:T(8,128)S(1)} dynamic-update-slice(f32[128,1024]{0,1:T(8,128)S(1)} %dynamic_update_slice.29, f32[16,1024]{0,1:T(8,128)} %collective-permute-done.6, s32[]{:T(128)S(6)} %select_n.142, s32[]{:T(128)} %constant.75.clone.1) | dynamic-update-slice | bytes 131076 | tf_op jit(solution)/shard_map/dynamic_update_slice | solution.py:22
  394.1 5.1 %collective-permute-done.7 = f32[16,1024]{0,1:T(8,128)S(1)} collective-permute-done((f32[16,1024]{0,1:T(8,128)}, f32[16,1024]{0,1:T(8,128)S(1)}, u32[]{:S(2)}, u32[]{:S(2)}) %collective-permute-start.7) | collective-permute-done | bytes 65568 | tf_op jit(solution)/shard_map/ppermute | solution.py:21
  399.1 3.0 dynamic_update_slice.31
  (61 shorter events, 35.6 us)
Async XLA Ops:
  6.5 1.9 copy-start.2
  6.5 33.8 %all-gather.2.cloned.1.call-start = ((), (), s32[]{:S(2)}) async-start(), calls=%async_computation.3 | async-start | bytes 25165824 | tf_op jit(solution)/shard_map/all_gather | solution.py:78
  7.3 94.8 %reduce-scatter.2.cloned.1.call-start = ((), (), s32[]{:S(2)}) async-start(), calls=%async_computation.4 | async-start | bytes 4718592 | tf_op jit(solution)/shard_map/reduce_scatter | solution.py:83
  40.4 14.5 %copy-start.5 = (bf16[1024,128]{1,0:T(8,128)(2,1)S(1)}, bf16[1024,128]{1,0:T(8,128)(2,1)}, u32[]{:S(2)}) copy-start(bf16[1024,128]{1,0:T(8,128)(2,1)} %param.8) | copy-start | bytes 786436
  54.8 7.2 %copy-start.6 = (f32[3,3,128]{2,1,0:T(4,128)S(1)}, f32[3,3,128]{2,1,0:T(4,128)}, u32[]{:S(2)}) copy-start(f32[3,3,128]{2,1,0:T(4,128)} %param.7) | copy-start | bytes 13828
  55.7 58.5 %all-to-all-start.1 = ((bf16[8,16,1024]{2,1,0:T(8,128)(2,1)}), bf16[8,16,1024]{2,1,0:T(8,128)(2,1)S(1)}, u32[]{:S(2)}, u32[]{:S(2)}) async-start(bf16[8,16,1024]{2,1,0:T(8,128)(2,1)} %bitcast.8), calls=%async_computation.2 | async-start | bytes 524288 | tf_op jit(solution)/shard_map/all_to_all | solution.py:111
  102.8 6.4 %collective-permute-start = (f32[2,384]{1,0:T(2,128)S(1)}, f32[2,384]{1,0:T(2,128)S(1)}, u32[]{:S(2)}, u32[]{:S(2)}) collective-permute-start(f32[2,384]{1,0:T(2,128)S(1)} %slice.79), channel_id=1, source_target_pairs={{0,2},{2,4},{4,6},{6,8},{8,10},{10,12},{12,14},{1,3},{3,5},{5,7},{... | collective-permute-start | bytes 9224 | tf_op jit(solution)/shard_map/ppermute | solution.py:29
  112.2 1.1 copy-start
  114.2 11.2 %all-to-all-start = ((bf16[8,16,1024]{2,1,0:T(8,128)(2,1)}), bf16[8,16,1024]{2,1,0:T(8,128)(2,1)S(1)}, u32[]{:S(2)}, u32[]{:S(2)}) async-start(bf16[8,16,1024]{2,1,0:T(8,128)(2,1)} %bitcast.5), calls=%async_computation.1 | async-start | bytes 524288 | tf_op jit(solution)/shard_map/all_to_all | solution.py:110
  303.4 13.6 %collective-permute-start.1 = (f32[16,1024]{0,1:T(8,128)S(1)}, f32[16,1024]{0,1:T(8,128)S(1)}, u32[]{:S(2)}, u32[]{:S(2)}) collective-permute-start(f32[16,1024]{0,1:T(8,128)S(1)} %get-tuple-element.11), channel_id=1, source_target_pairs={{0,2},{2,0},{4,6},{6,4},{8,10},{10,8},{12,14},{14,12},{1,3},{3,1},... | collective-permute-start | bytes 196616 | tf_op jit(solution)/shard_map/ppermute | solution.py:21
  303.6 34.0 %collective-permute-start.2 = (f32[16,1024]{0,1:T(8,128)S(1)}, f32[16,1024]{0,1:T(8,128)S(1)}, u32[]{:S(2)}, u32[]{:S(2)}) collective-permute-start(f32[16,1024]{0,1:T(8,128)S(1)} %get-tuple-element.10), channel_id=1, source_target_pairs={{0,4},{2,6},{4,0},{6,2},{8,12},{10,14},{12,8},{14,10},{1,5},{3,7},... | collective-permute-start | bytes 196616 | tf_op jit(solution)/shard_map/ppermute | solution.py:21
  305.8 44.9 %collective-permute-start.3 = (f32[16,1024]{0,1:T(8,128)}, f32[16,1024]{0,1:T(8,128)}, u32[]{:S(2)}, u32[]{:S(2)}) collective-permute-start(f32[16,1024]{0,1:T(8,128)} %get-tuple-element.9), channel_id=1, source_target_pairs={{0,6},{2,4},{4,2},{6,0},{8,14},{10,12},{12,10},{14,8},{1,7},{3,5},... | collective-permute-start | bytes 196616 | tf_op jit(solution)/shard_map/ppermute | solution.py:21
  306.9 48.3 %collective-permute-start.4 = (f32[16,1024]{0,1:T(8,128)}, f32[16,1024]{0,1:T(8,128)}, u32[]{:S(2)}, u32[]{:S(2)}) collective-permute-start(f32[16,1024]{0,1:T(8,128)} %get-tuple-element.8), channel_id=1, source_target_pairs={{0,8},{2,10},{4,12},{6,14},{8,0},{10,2},{12,4},{14,6},{1,9},{3,11}... | collective-permute-start | bytes 196616 | tf_op jit(solution)/shard_map/ppermute | solution.py:21
  309.0 68.9 %collective-permute-start.5 = (f32[16,1024]{0,1:T(8,128)}, f32[16,1024]{0,1:T(8,128)}, u32[]{:S(2)}, u32[]{:S(2)}) collective-permute-start(f32[16,1024]{0,1:T(8,128)} %get-tuple-element.7), channel_id=1, source_target_pairs={{0,10},{2,8},{4,14},{6,12},{8,2},{10,0},{12,6},{14,4},{1,11},{3,9}... | collective-permute-start | bytes 196616 | tf_op jit(solution)/shard_map/ppermute | solution.py:21
  317.0 20.6 %copy-start.3 = (f32[16,1024]{0,1:T(8,128)}, f32[16,1024]{0,1:T(8,128)S(1)}, u32[]{:S(2)}) copy-start(f32[16,1024]{0,1:T(8,128)S(1)} %collective-permute-done.1) | copy-start | bytes 196612
  317.0 72.6 %collective-permute-start.6 = (f32[16,1024]{0,1:T(8,128)}, f32[16,1024]{0,1:T(8,128)}, u32[]{:S(2)}, u32[]{:S(2)}) collective-permute-start(f32[16,1024]{0,1:T(8,128)} %get-tuple-element.6), channel_id=1, source_target_pairs={{0,12},{2,14},{4,8},{6,10},{8,4},{10,6},{12,0},{14,2},{1,13},{3,15... | collective-permute-start | bytes 196616 | tf_op jit(solution)/shard_map/ppermute | solution.py:21
  337.6 0.8 copy-start.4
  338.4 60.7 %collective-permute-start.7 = (f32[16,1024]{0,1:T(8,128)}, f32[16,1024]{0,1:T(8,128)S(1)}, u32[]{:S(2)}, u32[]{:S(2)}) collective-permute-start(f32[16,1024]{0,1:T(8,128)} %get-tuple-element.5), channel_id=1, source_target_pairs={{0,14},{2,12},{4,10},{6,8},{8,6},{10,4},{12,2},{14,0},{1,15},{3,13... | collective-permute-start | bytes 196616 | tf_op jit(solution)/shard_map/ppermute | solution.py:21
  338.6 63.5 %copy-start.1 = (f32[1024,384]{1,0:T(8,128)S(1)}, f32[1024,384]{1,0:T(8,128)}, u32[]{:S(2)}) copy-start(f32[1024,384]{1,0:T(8,128)} %copy-done) | copy-start | bytes 4718596
  338.6 63.5 %copy-start.7 = (f32[128]{0:T(128)S(1)}, f32[128]{0:T(128)}, u32[]{:S(2)}) copy-start(f32[128]{0:T(128)} %param.9) | copy-start | bytes 1540
Sparse Core Ops, SparseCore 0:
  8.9 31.3 all-gather.1
  55.0 47.0 reduce-scatter.1
